TPU v7x, 32 devices: a whole 2x2x4 slice. The times are simulated.
32 devices in a mesh: freq: 8 (over z, core), mode: 4 (over y, x).
Axes of the slice: x: 2, y: 2, z: 4, core: 2. Of those that a mesh axis runs over, the one named last changes fastest.
Arguments:
- sources: bfloat16 [16, 512, 2, 4096], P(None, None, None, ('freq', 'mode')), may hold values from -6 to 6
- mapping: bfloat16 [16, 2, 2048, 4096], P('freq', None, 'mode'), may hold values from -0.0625 to 0.0625
Outputs:
- pressure: bfloat16 [16, 512, 2, 2048], P(None, 'freq', None, 'mode')
All inputs are finite; a program needn't handle non-finite values.
Results may differ from a plain program's by a relative error of at most 0.0006.
Values may be sent and summed in bfloat16 or wider, within the bound.
A program may use at most 128 MiB of HBM per device.

v0:
```python
import jax
import jax.numpy as jnp
from jax import lax
from jax.sharding import PartitionSpec as P


def body(sources, mapping):
    freq_count = lax.axis_size("freq")
    mode_count = lax.axis_size("mode")
    bin_count = mapping.shape[0]
    slice_width = sources.shape[3]
    regrouped = lax.all_to_all(sources, "freq", split_axis=0, concat_axis=3, tiled=True)
    snapshots = regrouped.shape[1]
    blocked = regrouped.reshape(bin_count, snapshots, 2, 1, freq_count, slice_width)
    gathered = lax.all_gather(blocked, "mode", axis=3, tiled=True)
    complete = jnp.swapaxes(gathered, 3, 4).reshape(bin_count, snapshots, 2, -1)
    real_part = jnp.einsum(
        "bsm,bom->bso", complete[:, :, 0], mapping[:, 0], preferred_element_type=jnp.float32
    ) - jnp.einsum(
        "bsm,bom->bso", complete[:, :, 1], mapping[:, 1], preferred_element_type=jnp.float32
    )
    imag_part = jnp.einsum(
        "bsm,bom->bso", complete[:, :, 1], mapping[:, 0], preferred_element_type=jnp.float32
    ) + jnp.einsum(
        "bsm,bom->bso", complete[:, :, 0], mapping[:, 1], preferred_element_type=jnp.float32
    )
    field = jnp.stack([real_part, imag_part], axis=2)
    bins_total = bin_count * freq_count
    first_bin = lax.axis_index("freq") * bin_count
    bin_index = (first_bin + jnp.arange(bin_count, dtype=jnp.int32)).astype(jnp.float32)
    weights = ((bin_index + 1.0) / bins_total) ** 2
    local_energy = jnp.sum(weights[:, None, None, None] * field * field)
    energy = lax.psum(local_energy, ("freq", "mode"))
    energy = energy / (field.shape[1] * field.shape[3] * mode_count)
    factor = jnp.sqrt(bins_total / (energy + 1e-06))
    result = lax.all_to_all(
        (field * factor).astype(jnp.bfloat16), "freq", split_axis=1, concat_axis=0, tiled=True
    )
    return result


def solution(mesh):
    placed = (P(None, None, None, ("freq", "mode")), P("freq", None, "mode", None))
    return jax.shard_map(
        body, mesh=mesh, in_specs=placed, out_specs=P(None, "freq", None, "mode"), check_vma=False
    )
```

profile of v0, /device:TPU:0, one launch (start us, length us, event | category | flops | bytes accessed | tf_op | source)
XLA Modules:
  0.0 473.3 jit_solution(15611076914805232381)
XLA Ops:
  6.5 0.0 all-gather.3.cloned.1.call-start
  6.5 3.2 copy.16
  9.7 100.2 %all_to_all.33 = bf16[16,512,2,128]{3,1,2,0:T(8,128)(2,1)} all-to-all(bf16[16,512,2,128]{3,1,2,0:T(8,128)(2,1)S(1)} %copy.16), channel_id=1, replica_groups=mesh['freq'=8,'mode'=4] {'freq'}, dimensions={0} | all-to-all | bytes 8388608 | tf_op jit(solution)/shard_map/all_to_all | solution.py:12
  110.0 0.0 all-gather.3.cloned.1.call-update
  110.0 156.4 %all-gather.3.cloned.1.call-done = bf16[2,512,2,32,128]{4,1,2,0,3:T(8,128)(2,1)} async-done(((bf16[2,512,2,8,128]{4,1,2,0,3:T(8,128)(2,1)}), bf16[2,512,2,32,128]{4,1,2,0,3:T(8,128)(2,1)}) %all-gather.3.cloned.1.call-update) | async-done | bytes 16777232 | tf_op jit(solution)/shard_map/all_gather | solution.py:15
  266.4 22.3 %copy.18 = bf16[2,512,2,8,4,128]{5,4,3,1,0,2:T(4,128)(2,1)} copy(bf16[2,512,2,8,4,128]{5,1,2,0,3,4:T(8,128)(2,1)} %bitcast.46) | data formatting | bytes 33554432 | tf_op jit(solution)/shard_map/transpose | solution.py:16
  288.6 27.7 %reshape.16 = bf16[2,512,2,4096]{3,1,0,2:T(8,128)(2,1)} reshape(bf16[2,512,2,8,4,128]{5,4,3,1,0,2:T(4,128)(2,1)} %copy.18) | data formatting | bytes 33554432 | tf_op jit(solution)/shard_map/reshape | solution.py:16
  316.3 11.6 %fusion.2 = f32[2,512,512]{2,1,0:T(8,128)} fusion(bf16[2,512,2,4096]{3,1,0,2:T(8,128)(2,1)} %reshape.16, bf16[2,2,512,4096]{3,2,1,0:T(8,128)(2,1)} %param.3), kind=kOutput, calls=%fused_computation.4 | convolution fusion | flops 4294967296 | bytes 18874368 | tf_op jit(solution)/shard_map/bsm,bom->bso/dot_general | solution.py:19
  328.0 11.6 %fusion = f32[2,512,512]{2,1,0:T(8,128)} fusion(bf16[2,512,2,4096]{3,1,0,2:T(8,128)(2,1)} %reshape.16, bf16[2,2,512,4096]{3,2,1,0:T(8,128)(2,1)} %param.3), kind=kOutput, calls=%fused_computation.2 | convolution fusion | flops 4294967296 | bytes 18874368 | tf_op jit(solution)/shard_map/bsm,bom->bso/dot_general | solution.py:24
  339.6 10.9 %subtract_bitcast_fusion = f32[2,512,1,512]{3,1,0,2:T(8,128)S(1)} fusion(f32[2,512,512]{2,1,0:T(8,128)} %fusion.2, bf16[2,2,512,4096]{3,2,1,0:T(8,128)(2,1)} %param.3, bf16[2,512,2,4096]{3,1,0,2:T(8,128)(2,1)} %reshape.16), kind=kOutput, calls=%fused_computation.19 | convolution fusion | flops 4295491584 | bytes 20971520 | tf_op jit(solution)/shard_map/bsm,bom->bso/dot_general | solution.py:17
  350.4 12.4 %add_bitcast_fusion = f32[2,512,1,512]{3,1,0,2:T(8,128)} fusion(f32[2,512,512]{2,1,0:T(8,128)} %fusion, bf16[2,2,512,4096]{3,2,1,0:T(8,128)(2,1)} %param.3, bf16[2,512,2,4096]{3,1,0,2:T(8,128)(2,1)} %reshape.16), kind=kOutput, calls=%fused_computation.18 | convolution fusion | flops 4295491584 | bytes 20971520 | tf_op jit(solution)/shard_map/bsm,bom->bso/dot_general | solution.py:22
  362.9 3.4 fusion.12
  366.3 39.5 %psum.7 = f32[]{:T(128)} all-reduce(f32[]{:T(128)} %fusion.12), channel_id=1, replica_groups=mesh['freq'=8,'mode'=4] {'freq','mode'}, use_global_device_ids=true, to_apply=%region_1.0 | all-reduce | flops 1 | bytes 8 | tf_op jit(solution)/shard_map/psum | solution.py:33
  406.6 2.2 multiply_convert_fusion
  408.8 2.2 copy.21
  410.9 52.4 %all_to_all.34 = bf16[2,512,2,512]{3,0,2,1:T(2,128)(2,1)S(1)} all-to-all(bf16[2,512,2,512]{3,0,2,1:T(2,128)(2,1)S(1)} %copy.21), channel_id=1, replica_groups=mesh['freq'=8,'mode'=4] {'freq'}, dimensions={1} | all-to-all | bytes 4194304 | tf_op jit(solution)/shard_map/all_to_all | solution.py:36
  463.3 3.2 copy.22
  (1 shorter events, 0.0 us)
Async XLA Ops:
  6.5 259.8 %all-gather.3.cloned.1.call-start = ((), (), s32[]{:S(2)}) async-start(), calls=%async_computation.2 | async-start | bytes 20971520 | tf_op jit(solution)/shard_map/all_gather | solution.py:15
Sparse Core Ops, SparseCore 0:
  110.1 156.2 all-gather.2
where the time goes:
time: 474 us; the launch traced here: 473 us
  blocking collectives  192 us (41%)
  waiting for transfers between devices  156 us (33%)
  local copies, waits for them, and re-layouts  58.5 us (12%)
  matrix products  46.6 us (10%)
  between operations  14.2 us (3%)
  other arithmetic  5.6 us (1%)
    all_gather x1, waiting for transfers between devices, body(): gathered = lax.all_gather(blocked, 'mode', axis=3, tiled=True)  156 us
    all_to_all x1, blocking collectives, body(): lax.all_to_all(sources, 'freq', split_axis=0, concat_axis=3, tiled=True)  100 us
    all_to_all x1, blocking collectives, body(): lax.all_to_all((field * factor).astype(jnp.bfloat16), 'freq', split_axis=...  52.4 us
    psum x1, blocking collectives, body(): energy = lax.psum(local_energy, ('freq', 'mode'))  39.5 us
    reshape x1, local copies, waits for them, and re-layouts, body(): complete = jnp.swapaxes(gathered, 3, 4).reshape(bin_count, snapshots, 2, -1)  27.7 us
    transpose x1, local copies, waits for them, and re-layouts, body(): complete = jnp.swapaxes(gathered, 3, 4).reshape(bin_count, snapshots, 2, -1)  22.3 us
    dot_general x1, matrix products, body(): jnp.einsum('bsm,bom->bso', complete[:, :, 1], mapping[:, 0], preferred_el...  12.4 us
    dot_general x1, matrix products, body(): jnp.einsum('bsm,bom->bso', complete[:, :, 1], mapping[:, 1], preferred_el...  11.6 us
  transfers between devices with their start and end apart: 1, of which 1 were waited for; matrix products, arithmetic and copies ran while one was open for 0% of the time, Pallas kernels for 0%

commit v1 on v0

--- a/solution.py
+++ b/solution.py
@@ -12,7 +12,9 @@
     regrouped = lax.all_to_all(sources, "freq", split_axis=0, concat_axis=3, tiled=True)
     snapshots = regrouped.shape[1]
     blocked = regrouped.reshape(bin_count, snapshots, 2, 1, freq_count, slice_width)
-    gathered = lax.all_gather(blocked, "mode", axis=3, tiled=True)
+    gathered = jnp.concatenate(
+        lax.all_to_all(jnp.stack([blocked] * lax.axis_size("mode")), "mode", 0, 0), axis=3
+    )
     complete = jnp.swapaxes(gathered, 3, 4).reshape(bin_count, snapshots, 2, -1)
     real_part = jnp.einsum(
         "bsm,bom->bso", complete[:, :, 0], mapping[:, 0], preferred_element_type=jnp.float32

time: 474 us -> 516 us (1.089)
  waiting for transfers between devices: 156 us -> 182 us
  local copies, waits for them, and re-layouts: 58.5 us -> 81.9 us
  between operations: 14.2 us -> 0.82 us
  starting transfers between devices: 0.01 us -> 6.96 us
    all_to_all x0 -> x1, waiting for transfers between devices: none -> 182 us  [body(): lax.all_to_all(jnp.stack([blocked] * lax.axis_size('mode')), 'mode', 0, 0)]
    all_gather x1 -> x0, waiting for transfers between devices: 156 us -> none  [body(): gathered = lax.all_gather(blocked, 'mode', axis=3, tiled=True)]
    transpose x1, local copies, waits for them, and re-layouts: 22.3 us -> 40.2 us  [body(): complete = jnp.swapaxes(gathered, 3, 4).reshape(bin_count, snapshots, 2, -1)]
    all_to_all x0 -> x1, starting transfers between devices: none -> 6.96 us  [body(): lax.all_to_all(jnp.stack([blocked] * lax.axis_size('mode')), 'mode', 0, 0)]
    another operation x0 -> x1, local copies, waits for them, and re-layouts: none -> 5.98 us  [body(): jnp.stack([blocked] * lax.axis_size('mode'))]
where the time goes in v1:
time: 516 us; the launch traced here: 515 us
  blocking collectives  191 us (37%)
  waiting for transfers between devices  182 us (35%)
  local copies, waits for them, and re-layouts  81.9 us (16%)
  matrix products  46.6 us (9%)
  starting transfers between devices  6.96 us (1%)
  other arithmetic  5.6 us (1%)
    all_to_all x1, waiting for transfers between devices, body(): lax.all_to_all(jnp.stack([blocked] * lax.axis_size('mode')), 'mode', 0, 0)  182 us
    all_to_all x1, blocking collectives, body(): lax.all_to_all(sources, 'freq', split_axis=0, concat_axis=3, tiled=True)  100 us
    all_to_all x1, blocking collectives, body(): lax.all_to_all((field * factor).astype(jnp.bfloat16), 'freq', split_axis=...  52.9 us
    transpose x1, local copies, waits for them, and re-layouts, body(): complete = jnp.swapaxes(gathered, 3, 4).reshape(bin_count, snapshots, 2, -1)  40.2 us
    psum x1, blocking collectives, body(): energy = lax.psum(local_energy, ('freq', 'mode'))  37.5 us
    reshape x1, local copies, waits for them, and re-layouts, body(): complete = jnp.swapaxes(gathered, 3, 4).reshape(bin_count, snapshots, 2, -1)  27.7 us
    dot_general x1, matrix products, body(): jnp.einsum('bsm,bom->bso', complete[:, :, 1], mapping[:, 0], preferred_el...  12.4 us
    dot_general x1, matrix products, body(): jnp.einsum('bsm,bom->bso', complete[:, :, 1], mapping[:, 1], preferred_el...  11.6 us
  transfers between devices with their start and end apart: 1, of which 1 were waited for; matrix products, arithmetic and copies ran while one was open for 0% of the time, Pallas kernels for 0%

profile of v1, /device:TPU:0, one launch (start us, length us, event | category | flops | bytes accessed | tf_op | source)
XLA Modules:
  0.0 514.7 jit_solution(1200871743037257658)
XLA Ops:
  0.0 100.3 %all_to_all.38 = bf16[16,512,2,128]{3,2,1,0:T(2,128)(2,1)S(1)} all-to-all(bf16[16,512,2,128]{3,2,1,0:T(2,128)(2,1)} %param.2), channel_id=1, replica_groups=mesh['freq'=8,'mode'=4] {'freq'}, dimensions={0} | all-to-all | bytes 8388608 | tf_op jit(solution)/shard_map/all_to_all | solution.py:12
  100.3 2.7 copy.16
  103.0 6.0 %stack.12 = bf16[4,2,512,2,1,8,128]{6,5,2,1,3,4,0:T(8,128)(2,1)} broadcast(bf16[2,512,2,8,128]{4,3,1,0,2:T(8,128)(2,1)S(1)} %bitcast.49), dimensions={1,2,3,5,6} | broadcast | bytes 20971520 | tf_op jit(solution)/shard_map/stack | solution.py:16
  109.0 7.0 %all-to-all-start.1 = ((bf16[4,2,512,2,1,8,128]{6,5,2,1,3,4,0:T(8,128)(2,1)}), bf16[4,2,512,2,1,8,128]{6,5,2,1,3,4,0:T(8,128)(2,1)}, u32[]{:S(2)}, u32[]{:S(2)}) async-start(bf16[4,2,512,2,1,8,128]{6,5,2,1,3,4,0:T(8,128)(2,1)} %stack.12), calls=%async_computation.1 | async-start | bytes 33554432 | tf_op jit(solution)/shard_map/all_to_all | solution.py:16
  116.0 182.1 %all-to-all-done.1 = bf16[4,2,512,2,1,8,128]{6,5,2,1,3,4,0:T(8,128)(2,1)} async-done(((bf16[4,2,512,2,1,8,128]{6,5,2,1,3,4,0:T(8,128)(2,1)}), bf16[4,2,512,2,1,8,128]{6,5,2,1,3,4,0:T(8,128)(2,1)}, u32[]{:S(2)}, u32[]{:S(2)}) %all-to-all-start.1) | async-done | bytes 16777248 | tf_op jit(solution)/shard_map/all_to_all | solution.py:16
  298.1 40.2 %copy.8 = bf16[2,512,2,8,4,128]{5,4,3,1,0,2:T(4,128)(2,1)} copy(bf16[2,512,2,8,4,128]{5,3,1,0,2,4:T(8,128)(2,1)} %bitcast.4) | data formatting | bytes 33554432 | tf_op jit(solution)/shard_map/transpose | solution.py:18
  338.4 27.7 %reshape.22 = bf16[2,512,2,4096]{3,1,0,2:T(8,128)(2,1)} reshape(bf16[2,512,2,8,4,128]{5,4,3,1,0,2:T(4,128)(2,1)} %copy.8) | data formatting | bytes 33554432 | tf_op jit(solution)/shard_map/reshape | solution.py:18
  366.0 11.6 %fusion.2 = f32[2,512,512]{2,1,0:T(8,128)} fusion(bf16[2,512,2,4096]{3,1,0,2:T(8,128)(2,1)} %reshape.22, bf16[2,2,512,4096]{3,2,1,0:T(8,128)(2,1)} %param.3), kind=kOutput, calls=%fused_computation.4 | convolution fusion | flops 4294967296 | bytes 18874368 | tf_op jit(solution)/shard_map/bsm,bom->bso/dot_general | solution.py:21
  377.7 11.6 %fusion = f32[2,512,512]{2,1,0:T(8,128)} fusion(bf16[2,512,2,4096]{3,1,0,2:T(8,128)(2,1)} %reshape.22, bf16[2,2,512,4096]{3,2,1,0:T(8,128)(2,1)} %param.3), kind=kOutput, calls=%fused_computation.2 | convolution fusion | flops 4294967296 | bytes 18874368 | tf_op jit(solution)/shard_map/bsm,bom->bso/dot_general | solution.py:26
  389.3 10.9 %subtract_bitcast_fusion = f32[2,512,1,512]{3,1,0,2:T(8,128)S(1)} fusion(f32[2,512,512]{2,1,0:T(8,128)} %fusion.2, bf16[2,2,512,4096]{3,2,1,0:T(8,128)(2,1)} %param.3, bf16[2,512,2,4096]{3,1,0,2:T(8,128)(2,1)} %reshape.22), kind=kOutput, calls=%fused_computation.20 | convolution fusion | flops 4295491584 | bytes 20971520 | tf_op jit(solution)/shard_map/bsm,bom->bso/dot_general | solution.py:19
  400.2 12.4 %add_bitcast_fusion = f32[2,512,1,512]{3,1,0,2:T(8,128)} fusion(f32[2,512,512]{2,1,0:T(8,128)} %fusion, bf16[2,2,512,4096]{3,2,1,0:T(8,128)(2,1)} %param.3, bf16[2,512,2,4096]{3,1,0,2:T(8,128)(2,1)} %reshape.22), kind=kOutput, calls=%fused_computation.19 | convolution fusion | flops 4295491584 | bytes 20971520 | tf_op jit(solution)/shard_map/bsm,bom->bso/dot_general | solution.py:24
  412.6 3.4 fusion.12
  416.0 37.5 %psum.7 = f32[]{:T(128)} all-reduce(f32[]{:T(128)} %fusion.12), channel_id=1, replica_groups=mesh['freq'=8,'mode'=4] {'freq','mode'}, use_global_device_ids=true, to_apply=%region_1.0 | all-reduce | flops 1 | bytes 8 | tf_op jit(solution)/shard_map/psum | solution.py:35
  454.4 2.2 multiply_convert_fusion
  456.5 2.2 copy.11
  458.7 52.9 %all_to_all.39 = bf16[2,512,2,512]{3,0,2,1:T(2,128)(2,1)S(1)} all-to-all(bf16[2,512,2,512]{3,0,2,1:T(2,128)(2,1)S(1)} %copy.11), channel_id=1, replica_groups=mesh['freq'=8,'mode'=4] {'freq'}, dimensions={1} | all-to-all | bytes 4194304 | tf_op jit(solution)/shard_map/all_to_all | solution.py:38
  511.6 3.2 copy.12
  (1 shorter events, 0.0 us)
Async XLA Ops:
  109.0 189.1 %all-to-all-start.1 = ((bf16[4,2,512,2,1,8,128]{6,5,2,1,3,4,0:T(8,128)(2,1)}), bf16[4,2,512,2,1,8,128]{6,5,2,1,3,4,0:T(8,128)(2,1)}, u32[]{:S(2)}, u32[]{:S(2)}) async-start(bf16[4,2,512,2,1,8,128]{6,5,2,1,3,4,0:T(8,128)(2,1)} %stack.12), calls=%async_computation.1 | async-start | bytes 33554432 | tf_op jit(solution)/shard_map/all_to_all | solution.py:16
